TPU v7x, 32 devices: a whole 2x2x4 slice. The times are simulated.
32 devices in a mesh: bx: 8 (over z, x), by: 4 (over y, core).
Axes of the slice: x: 2, y: 2, z: 4, core: 2. Of those that a mesh axis runs over, the one named last changes fastest.
Arguments:
- box_map: float32 [8, 4, 256, 256], P('bx', 'by'), as said below
- box_load: float32 [8, 4, 64, 256], P('bx', 'by'), may hold values from -6 to 6
- box_order: int32 [8, 4, 256], P('bx', 'by'), may hold values from 0 to 255, each once within a row
- incoming: float32 [8, 4, 64, 128], P('bx', 'by'), may hold values from -54 to 54
- edge_map: float32 [8, 4, 256, 128], P('bx', 'by'), may hold values from -0.375 to 0.375
- edge_load: float32 [8, 4, 64, 128], P('bx', 'by'), may hold values from -6 to 6
Outputs:
- top_map: float32 [8, 4, 512, 128], P('bx', 'by')
- top_load: float32 [8, 4, 64, 128], P('bx', 'by')
- box_incoming: float32 [8, 4, 64, 256], P('bx', 'by')
- edge_values: float32 [8, 4, 64, 128], P('bx', 'by')
Inputs may be any that keep to these rules, and one draw needn't show every extreme that they name: Each row of box_order holds every number from 0 to 255 once. Every box_map[i, j] has spectral norm at most 0.7.
All inputs are finite; a program needn't handle non-finite values.
Results may differ from a plain program's by a relative error of at most 0.0001.
Values sent between devices are 32-bit elements; how exact they have to be, the bound alone decides.
No kernel may reach another device: no remote copies, remote signals or barrier semaphores. Data moves between devices by JAX's collectives and lax.ppermute only.
A program may use at most 64 MiB of HBM per device.

v0:
```python
import jax
import jax.numpy as jnp
from jax import lax
from jax.sharding import PartitionSpec as P

ALPHA_ORDER = ((0, 2, 3, 1), (0, 3, 2, 1))
BETA_ORDER = ((1, 2, 3, 0), (1, 3, 2, 0))
MACRO_ORDER = (0, 1, 3, 4, 2, 5)


def swapped(block, axis, apart):
    count = lax.axis_size(axis)
    route = []
    for low in range(count):
        high = low | 1 << apart
        if high != low and high < count:
            route += [(low, high), (high, low)]
    return lax.ppermute(block, axis, route)


def matmul(first, second):
    return jnp.dot(
        first, second, precision=lax.Precision.HIGHEST, preferred_element_type=jnp.float32
    )


def block_index(blocks, breadth):
    return jnp.concatenate(
        [jnp.arange(breadth, dtype=jnp.int32) + number * breadth for number in blocks]
    )


def canonical_blocks(order):
    return tuple((order.index(number) for number in range(4)))


def inverse_of(kernel):
    normal_matrix = matmul(kernel.T, kernel)
    factor = jnp.linalg.cholesky(normal_matrix)
    return jax.scipy.linalg.cho_solve((factor, True), kernel.T)


def interface_terms(alpha_outer, alpha_inner, alpha_free, beta_outer, beta_inner, beta_free):
    inner_size = alpha_inner.shape[0]
    kernel = jnp.eye(inner_size, dtype=jnp.float32) - matmul(beta_inner, alpha_inner)
    inverse = inverse_of(kernel)
    alpha_from_alpha = matmul(alpha_outer, inverse)
    alpha_from_beta = -matmul(matmul(beta_outer, alpha_inner), inverse)
    alpha_source = matmul(alpha_free - matmul(beta_free, alpha_inner), inverse)
    beta_from_alpha = -matmul(alpha_from_alpha, beta_inner)
    beta_from_beta = beta_outer - matmul(alpha_from_beta, beta_inner)
    beta_source = beta_free - matmul(alpha_source, beta_inner)
    return (
        alpha_from_alpha,
        alpha_from_beta,
        alpha_source,
        beta_from_alpha,
        beta_from_beta,
        beta_source,
    )


def full_merge(alpha_map, alpha_load, beta_map, beta_load, outer):
    terms = interface_terms(
        alpha_map[:outer, outer:],
        alpha_map[outer:, outer:],
        alpha_load[:, outer:],
        beta_map[:outer, outer:],
        beta_map[outer:, outer:],
        beta_load[:, outer:],
    )
    (
        alpha_from_alpha,
        alpha_from_beta,
        alpha_source,
        beta_from_alpha,
        beta_from_beta,
        beta_source,
    ) = terms
    alpha_back = alpha_map[outer:, :outer]
    beta_back = beta_map[outer:, :outer]
    upper = jnp.concatenate(
        [
            alpha_map[:outer, :outer] - matmul(beta_from_alpha, alpha_back),
            -matmul(alpha_from_alpha, beta_back),
        ],
        axis=1,
    )
    lower = jnp.concatenate(
        [
            -matmul(beta_from_beta, alpha_back),
            beta_map[:outer, :outer] - matmul(alpha_from_beta, beta_back),
        ],
        axis=1,
    )
    merged = jnp.concatenate([upper, lower], axis=0)
    merged_load = jnp.concatenate(
        [
            alpha_load[:, :outer] - matmul(beta_source, alpha_back),
            beta_load[:, :outer] - matmul(alpha_source, beta_back),
        ],
        axis=1,
    )
    return (merged, merged_load, terms)


def interface_values(terms, alpha_in, beta_in):
    (
        alpha_from_alpha,
        alpha_from_beta,
        alpha_source,
        beta_from_alpha,
        beta_from_beta,
        beta_source,
    ) = terms
    alpha_value = (
        matmul(alpha_in, alpha_from_alpha) + matmul(beta_in, alpha_from_beta) + alpha_source
    )
    beta_value = matmul(alpha_in, beta_from_alpha) + matmul(beta_in, beta_from_beta) + beta_source
    return (alpha_value, beta_value)


def body(box_map, box_load, box_order, incoming, edge_map, edge_load):
    own_map = box_map[0, 0]
    own_load = box_load[0, 0]
    own_order = box_order[0, 0]
    raw_incoming = incoming[0, 0]
    own_edge = edge_map[0, 0]
    own_edge_load = edge_load[0, 0]
    breadth = own_map.shape[0] // 4
    share_size = 2 * breadth
    outer = 4 * breadth
    box_total = lax.axis_size("bx") * lax.axis_size("by")
    power = lax.psum(jnp.sum(raw_incoming * raw_incoming, axis=1), ("bx", "by"))
    factor = 1.0 / jnp.sqrt(power / (box_total * raw_incoming.shape[1]) + 1e-06)
    own_incoming = raw_incoming * factor[:, None]
    x_parity = lax.axis_index("bx") % 2
    y_parity = lax.axis_index("by") % 2
    role_index = 2 * x_parity + y_parity
    is_alpha = x_parity == 0
    is_bottom = y_parity == 0
    forward_table = jnp.stack(
        [
            block_index(ALPHA_ORDER[0], breadth),
            block_index(ALPHA_ORDER[1], breadth),
            block_index(BETA_ORDER[0], breadth),
            block_index(BETA_ORDER[1], breadth),
        ]
    )
    picked = jnp.take(own_order, forward_table[role_index], axis=0)
    role_map = jnp.take(jnp.take(own_map, picked, axis=0), picked, axis=1)
    role_load = jnp.take(own_load, picked, axis=1)
    other_map, other_load, other_incoming = swapped((role_map, role_load, own_incoming), "bx", 0)
    alpha_map = jnp.where(is_alpha, role_map, other_map)
    beta_map = jnp.where(is_alpha, other_map, role_map)
    alpha_load = jnp.where(is_alpha, role_load, other_load)
    beta_load = jnp.where(is_alpha, other_load, role_load)
    alpha_incoming = jnp.where(is_alpha, own_incoming, other_incoming)
    beta_incoming = jnp.where(is_alpha, other_incoming, own_incoming)
    level_map, level_load, level_terms = full_merge(
        alpha_map, alpha_load, beta_map, beta_load, 3 * breadth
    )
    macro_index = block_index(MACRO_ORDER, breadth)
    macro_map = jnp.take(jnp.take(level_map, macro_index, axis=0), macro_index, axis=1)
    macro_load = jnp.take(level_load, macro_index, axis=1)
    macro_incoming = jnp.concatenate([alpha_incoming, beta_incoming], axis=1)
    far_outer, far_inner, far_free, far_incoming = swapped(
        (
            macro_map[:outer, outer:],
            macro_map[outer:, outer:],
            macro_load[:, outer:],
            macro_incoming,
        ),
        "by",
        0,
    )
    near_terms = interface_terms(
        macro_map[:outer, outer:],
        macro_map[outer:, outer:],
        macro_load[:, outer:],
        far_outer,
        far_inner,
        far_free,
    )
    near_value, far_value = interface_values(near_terms, macro_incoming, far_incoming)
    macro_inside = -far_value
    start = x_parity * share_size
    own_back = lax.dynamic_slice_in_dim(macro_map[outer:, :outer], start, share_size, 1)
    own_columns = lax.dynamic_slice_in_dim(macro_map[:outer, :outer], start, share_size, 1)
    near_rows = own_columns - matmul(near_terms[3], own_back)
    far_rows = -matmul(near_terms[4], own_back)
    top_share_map = jnp.where(
        is_bottom,
        jnp.concatenate([near_rows, far_rows], axis=0),
        jnp.concatenate([far_rows, near_rows], axis=0),
    )
    top_share_load = lax.dynamic_slice_in_dim(macro_load[:, :outer], start, share_size, 1) - matmul(
        near_terms[5], own_back
    )
    alpha_in = jnp.concatenate([macro_incoming[:, :share_size], macro_inside[:, :breadth]], axis=1)
    beta_in = jnp.concatenate([macro_incoming[:, share_size:], macro_inside[:, breadth:]], axis=1)
    alpha_value, beta_value = interface_values(level_terms, alpha_in, beta_in)
    role_values = jnp.where(
        is_alpha,
        jnp.concatenate([alpha_in, -beta_value], axis=1),
        jnp.concatenate([beta_in, -alpha_value], axis=1),
    )
    backward_table = jnp.stack(
        [
            block_index(canonical_blocks(ALPHA_ORDER[0]), breadth),
            block_index(canonical_blocks(ALPHA_ORDER[1]), breadth),
            block_index(canonical_blocks(BETA_ORDER[0]), breadth),
            block_index(canonical_blocks(BETA_ORDER[1]), breadth),
        ]
    )
    box_values = jnp.take(role_values, backward_table[role_index], axis=1)
    edge_values = matmul(box_values, own_edge) + own_edge_load
    return (
        top_share_map[None, None],
        top_share_load[None, None],
        box_values[None, None],
        edge_values[None, None],
    )


def solution(mesh):
    in_specs = (
        P("bx", "by", None, None),
        P("bx", "by", None, None),
        P("bx", "by", None),
        P("bx", "by", None, None),
        P("bx", "by", None, None),
        P("bx", "by", None, None),
    )
    out_specs = (
        P("bx", "by", None, None),
        P("bx", "by", None, None),
        P("bx", "by", None, None),
        P("bx", "by", None, None),
    )
    return jax.shard_map(body, mesh=mesh, in_specs=in_specs, out_specs=out_specs, check_vma=False)
```

profile of v0, /device:TPU:0, one launch (start us, length us, event | category | flops | bytes accessed | tf_op | source)
XLA Modules:
  0.0 114.0 jit_solution(9329707255149828205)
XLA Ops:
  1.1 0.7 copy-done.1
  1.8 1.9 %gather_fusion = s32[256]{0:T(256)S(1)} fusion(s32[256]{0:T(256)S(1)} %bitcast.135, s32[1024]{0:T(1024)S(1)} %pad_clamp_fusion.4), kind=kCustom, calls=%fused_computation.2 | custom fusion | bytes 3072 | tf_op jit(solution)/shard_map/jit(_take)/gather | solution.py:150
  3.8 1.0 gather_fusion.1
  4.9 1.0 gather_fusion.2
  6.1 3.0 %collective-permute-start = (f32[256,256]{1,0:T(8,128)S(1)}, f32[256,256]{1,0:T(8,128)S(1)}, u32[]{:S(2)}, u32[]{:S(2)}) collective-permute-start(f32[256,256]{1,0:T(8,128)S(1)} %select_bitcast_fusion.1), channel_id=1, source_target_pairs={{0,4},{4,0},{8,12},{12,8},{16,20},{20,16},{24,28},{28,24},{1,5},{5... | collective-permute-start | bytes 786440 | tf_op jit(solution)/shard_map/ppermute | solution.py:18
  9.2 0.7 gather_fusion.6
  10.1 0.8 collective-permute-start.3
  11.0 40.5 %psum.7 = f32[64]{0:T(128)S(1)} all-reduce(f32[64]{0:T(128)S(1)} %fusion.52), channel_id=1, replica_groups=mesh['bx'=8,'by'=4] {'bx','by'}, use_global_device_ids=true, to_apply=%region_5.7 | all-reduce | flops 64 | bytes 512 | tf_op jit(solution)/shard_map/psum | solution.py:134
  51.6 2.3 %collective-permute-start.5 = (f32[64,128]{1,0:T(8,128)S(1)}, f32[64,128]{1,0:T(8,128)S(1)}, u32[]{:S(2)}, u32[]{:S(2)}) collective-permute-start(f32[64,128]{1,0:T(8,128)S(1)} %bitcast_multiply_fusion), channel_id=1, source_target_pairs={{0,4},{4,0},{8,12},{12,8},{16,20},{20,16},{24,28},{28,24},{1,5},{5... | collective-permute-start | bytes 98312 | tf_op jit(solution)/shard_map/ppermute | solution.py:18
  54.1 1.6 %collective-permute-done.5 = f32[64,128]{1,0:T(8,128)S(1)} collective-permute-done((f32[64,128]{1,0:T(8,128)S(1)}, f32[64,128]{1,0:T(8,128)S(1)}, u32[]{:S(2)}, u32[]{:S(2)}) %collective-permute-start.5) | collective-permute-done | bytes 32800 | tf_op jit(solution)/shard_map/ppermute | solution.py:18
  56.8 5.8 %cholesky.31 = f32[64,64]{1,0:T(8,128)S(1)} custom-call(f32[64,64]{1,0:T(8,128)S(1)} %fusion.57), custom_call_target="Cholesky" | custom-call | tf_op jit(solution)/shard_map/jit(cholesky)/cholesky | solution.py:39
  62.7 0.6 compare_reduce_fusion.1
  63.3 0.7 fusion.50
  64.0 4.9 %custom-call.20 = f32[1,64,64]{1,2,0:T(8,128)S(1)} custom-call(f32[1,64,64]{2,1,0:T(8,128)S(1)} %fusion.50), custom_call_target="InvertDiagBlocksLowerTriangular" | custom-call | tf_op jit(solution)/shard_map/jit(_cho_solve)/triangular_solve | solution.py:40
  70.0 0.4 fusion.13
  71.7 0.4 convolution_subtract_fusion.2
  72.9 1.1 gather_fusion.5
  74.2 0.5 collective-permute-start.4
  75.6 1.7 %gather_fusion.3 = f32[384,384]{1,0:T(8,128)S(1)} fusion(f32[384,384]{1,0:T(8,128)S(1)} %maximum_maximum_fusion, s32[1024]{0:T(1024)S(1)} %pad_clamp_fusion.2), kind=kCustom, calls=%fused_computation.5 | custom fusion | bytes 1181184 | tf_op jit(solution)/shard_map/jit(_take)/gather | solution.py:164
  77.6 1.9 %gather_fusion.4 = f32[384,384]{1,0:T(8,128)S(1)} fusion(f32[384,384]{0,1:T(8,128)S(1)} %broadcast_select_fusion, s32[1024]{0:T(1024)S(1)} %pad_clamp_fusion.2), kind=kCustom, calls=%fused_computation.6 | custom fusion | bytes 1181184 | tf_op jit(solution)/shard_map/jit(_take)/gather | solution.py:164
  80.0 0.5 collective-permute-start.2
  80.7 0.5 collective-permute-done.1
  81.8 11.7 %cholesky.65 = f32[128,128]{1,0:T(8,128)S(1)} custom-call(f32[128,128]{1,0:T(8,128)S(1)} %fusion.24), custom_call_target="Cholesky" | custom-call | tf_op jit(solution)/shard_map/jit(cholesky)/cholesky | solution.py:39
  93.6 0.6 compare_reduce_fusion
  94.2 0.7 fusion.17
  94.9 9.8 %custom-call.21 = f32[1,128,128]{1,2,0:T(8,128)S(1)} custom-call(f32[1,128,128]{2,1,0:T(8,128)S(1)} %fusion.17), custom_call_target="InvertDiagBlocksLowerTriangular" | custom-call | tf_op jit(solution)/shard_map/jit(_cho_solve)/triangular_solve | solution.py:40
  106.1 0.6 slice-done
  106.7 0.8 fusion.9
  110.5 0.7 gather_fusion.7
  111.3 0.7 copy.35
  112.2 1.1 fusion.2
  113.3 0.7 maximum_select_fusion
  (125 shorter events, 12.5 us)
Async XLA Ops:
  0.6 3.1 %copy-start = (f32[1,1,256,256]{3,2,1,0:T(8,128)S(1)}, f32[1,1,256,256]{3,2,1,0:T(8,128)}, u32[]{:S(2)}) copy-start(f32[1,1,256,256]{3,2,1,0:T(8,128)} %param.8) | copy-start | bytes 786436
  1.1 0.7 copy-start.1
  6.0 3.1 %copy-start.5 = (f32[1,1,64,256]{3,2,1,0:T(8,128)S(1)}, f32[1,1,64,256]{3,2,1,0:T(8,128)}, u32[]{:S(2)}) copy-start(f32[1,1,64,256]{3,2,1,0:T(8,128)} %param.9) | copy-start | bytes 196612
  6.1 49.9 %collective-permute-start = (f32[256,256]{1,0:T(8,128)S(1)}, f32[256,256]{1,0:T(8,128)S(1)}, u32[]{:S(2)}, u32[]{:S(2)}) collective-permute-start(f32[256,256]{1,0:T(8,128)S(1)} %select_bitcast_fusion.1), channel_id=1, source_target_pairs={{0,4},{4,0},{8,12},{12,8},{16,20},{20,16},{24,28},{28,24},{1,5},{5... | collective-permute-start | bytes 786440 | tf_op jit(solution)/shard_map/ppermute | solution.py:18
  10.0 0.8 copy-start.3
  10.1 45.8 %collective-permute-start.3 = (f32[64,256]{1,0:T(8,128)S(1)}, f32[64,256]{1,0:T(8,128)S(1)}, u32[]{:S(2)}, u32[]{:S(2)}) collective-permute-start(f32[64,256]{1,0:T(8,128)S(1)} %select_bitcast_fusion.4), channel_id=1, source_target_pairs={{0,4},{4,0},{8,12},{12,8},{16,20},{20,16},{24,28},{28,24},{1,5},{5... | collective-permute-start | bytes 196616 | tf_op jit(solution)/shard_map/ppermute | solution.py:18
  51.6 4.2 %collective-permute-start.5 = (f32[64,128]{1,0:T(8,128)S(1)}, f32[64,128]{1,0:T(8,128)S(1)}, u32[]{:S(2)}, u32[]{:S(2)}) collective-permute-start(f32[64,128]{1,0:T(8,128)S(1)} %bitcast_multiply_fusion), channel_id=1, source_target_pairs={{0,4},{4,0},{8,12},{12,8},{16,20},{20,16},{24,28},{28,24},{1,5},{5... | collective-permute-start | bytes 98312 | tf_op jit(solution)/shard_map/ppermute | solution.py:18
  55.8 52.8 %collective-permute-start.6 = (f32[64,256]{1,0:T(8,128)S(1)}, f32[64,256]{1,0:T(8,128)S(1)}, u32[]{:S(2)}, u32[]{:S(2)}) collective-permute-start(f32[64,256]{1,0:T(8,128)S(1)} %pad_maximum_fusion.1), channel_id=1, source_target_pairs={{0,1},{1,0},{2,3},{3,2},{4,5},{5,4},{6,7},{7,6},{8,9},{9,8},{10,11... | collective-permute-start | bytes 196616 | tf_op jit(solution)/shard_map/ppermute | solution.py:18
  74.2 6.3 %copy-start.2 = (f32[64,384]{1,0:T(8,128)}, f32[64,384]{1,0:T(8,128)S(1)}, u32[]{:S(2)}) copy-start(f32[64,384]{1,0:T(8,128)S(1)} %select_bitcast_fusion.3) | copy-start | bytes 294916
  74.2 6.3 %collective-permute-start.4 = (f32[64,128]{1,0:T(8,128)S(1)}, f32[64,128]{1,0:T(8,128)S(1)}, u32[]{:S(2)}, u32[]{:S(2)}) collective-permute-start(f32[64,128]{1,0:T(8,128)S(1)} %slice.152), channel_id=1, source_target_pairs={{0,1},{1,0},{2,3},{3,2},{4,5},{5,4},{6,7},{7,6},{8,9},{9,8},{10,11... | collective-permute-start | bytes 98312 | tf_op jit(solution)/shard_map/ppermute | solution.py:18
  79.9 1.3 %collective-permute-start.1 = (f32[128,128]{1,0:T(8,128)S(1)}, f32[128,128]{1,0:T(8,128)S(1)}, u32[]{:S(2)}, u32[]{:S(2)}) collective-permute-start(f32[128,128]{1,0:T(8,128)S(1)} %slice.145), channel_id=1, source_target_pairs={{0,1},{1,0},{2,3},{3,2},{4,5},{5,4},{6,7},{7,6},{8,9},{9,8},{10,11... | collective-permute-start | bytes 196616 | tf_op jit(solution)/shard_map/ppermute | solution.py:18
  80.0 27.8 %collective-permute-start.2 = (f32[256,128]{1,0:T(8,128)S(1)}, f32[256,128]{1,0:T(8,128)S(1)}, u32[]{:S(2)}, u32[]{:S(2)}) collective-permute-start(f32[256,128]{1,0:T(8,128)S(1)} %slice.144), channel_id=1, source_target_pairs={{0,1},{1,0},{2,3},{3,2},{4,5},{5,4},{6,7},{7,6},{8,9},{9,8},{10,11... | collective-permute-start | bytes 393224 | tf_op jit(solution)/shard_map/ppermute | solution.py:18
  105.8 0.8 slice-start
  111.3 0.9 copy-start.4
  111.3 0.9 copy-start.6
where the time goes:
time: 114 us
  blocking collectives  40.5 us (36%)
  other arithmetic  37 us (32%)
  local copies, waits for them, and re-layouts  14 us (12%)
  matrix products  11.6 us (10%)
  starting transfers between devices  7.3 us (6%)
  waiting for transfers between devices  2.16 us (2%)
  between operations  1.44 us (1%)
    psum x1, blocking collectives, body(): power = lax.psum(jnp.sum(raw_incoming * raw_incoming, axis=1), ('bx', 'by'))  40.5 us
    another operation x6, other arithmetic, inverse_of(): factor = jnp.linalg.cholesky(normal_matrix)  18.9 us
    another operation x4, other arithmetic, inverse_of(): return jax.scipy.linalg.cho_solve((factor, True), kernel.T)  16 us
    dot_general x36, matrix products, matmul(): jnp.dot(first, second, precision=lax.Precision.HIGHEST, preferred_element...  10.7 us
    ppermute x7, starting transfers between devices, swapped(): return lax.ppermute(block, axis, route)  7.3 us
  transfers between devices with their start and end apart: 7, of which 2 were waited for; matrix products, arithmetic and copies ran while one was open for 45% of the time, Pallas kernels for 0%

commit v1 on v0

--- a/solution.py
+++ b/solution.py
@@ -131,7 +131,9 @@
     share_size = 2 * breadth
     outer = 4 * breadth
     box_total = lax.axis_size("bx") * lax.axis_size("by")
-    power = lax.psum(jnp.sum(raw_incoming * raw_incoming, axis=1), ("bx", "by"))
+    power = jnp.sum(
+        lax.all_gather(jnp.sum(raw_incoming * raw_incoming, axis=1), ("bx", "by")), axis=0
+    )
     factor = 1.0 / jnp.sqrt(power / (box_total * raw_incoming.shape[1]) + 1e-06)
     own_incoming = raw_incoming * factor[:, None]
     x_parity = lax.axis_index("bx") % 2

time: 114 us -> 115 us (level)
    psum x1 -> x0, blocking collectives: 40.5 us -> none  [body(): power = lax.psum(jnp.sum(raw_incoming * raw_incoming, axis=1), ('bx', 'by'))]
    unnamed x0 -> x1, blocking collectives: none -> 40.3 us
where the time goes in v1:
time: 115 us; the launch traced here: 114 us
  blocking collectives  40.3 us (35%)
  other arithmetic  37.1 us (32%)
  local copies, waits for them, and re-layouts  14.3 us (12%)
  matrix products  11.6 us (10%)
  starting transfers between devices  7.3 us (6%)
  waiting for transfers between devices  2.16 us (2%)
  between operations  1.46 us (1%)
    unnamed x1, blocking collectives  40.3 us
    another operation x6, other arithmetic, inverse_of(): factor = jnp.linalg.cholesky(normal_matrix)  18.9 us
    another operation x4, other arithmetic, inverse_of(): return jax.scipy.linalg.cho_solve((factor, True), kernel.T)  16 us
    dot_general x36, matrix products, matmul(): jnp.dot(first, second, precision=lax.Precision.HIGHEST, preferred_element...  10.7 us
    ppermute x7, starting transfers between devices, swapped(): return lax.ppermute(block, axis, route)  7.3 us
  transfers between devices with their start and end apart: 7, of which 2 were waited for; matrix products, arithmetic and copies ran while one was open for 45% of the time, Pallas kernels for 0%

profile of v1, /device:TPU:0, one launch (start us, length us, event | category | flops | bytes accessed | tf_op | source)
XLA Modules:
  0.0 114.3 jit_solution(4507893138901487593)
XLA Ops:
  1.1 0.7 copy-done.1
  1.8 1.9 %gather_fusion = s32[256]{0:T(256)S(1)} fusion(s32[256]{0:T(256)S(1)} %bitcast.135, s32[1024]{0:T(1024)S(1)} %pad_clamp_fusion.4), kind=kCustom, calls=%fused_computation.2 | custom fusion | bytes 3072 | tf_op jit(solution)/shard_map/jit(_take)/gather | solution.py:152
  3.8 1.0 gather_fusion.1
  4.9 1.0 gather_fusion.2
  6.1 3.0 %collective-permute-start = (f32[256,256]{1,0:T(8,128)S(1)}, f32[256,256]{1,0:T(8,128)S(1)}, u32[]{:S(2)}, u32[]{:S(2)}) collective-permute-start(f32[256,256]{1,0:T(8,128)S(1)} %select_bitcast_fusion.1), channel_id=1, source_target_pairs={{0,4},{4,0},{8,12},{12,8},{16,20},{20,16},{24,28},{28,24},{1,5},{5... | collective-permute-start | bytes 786440 | tf_op jit(solution)/shard_map/ppermute | solution.py:18
  9.2 0.7 gather_fusion.6
  10.1 0.8 collective-permute-start.3
  11.3 40.3 %all-reduce = f32[2048]{0:T(1024)S(1)} all-reduce(f32[2048]{0:T(1024)S(1)} %dynamic-update-slice.6), channel_id=2, replica_groups=mesh['bx'=8,'by'=4] {'bx','by'}, use_global_device_ids=true, to_apply=%add | all-reduce | flops 2048 | bytes 16384
  51.8 2.3 %collective-permute-start.5 = (f32[64,128]{1,0:T(8,128)S(1)}, f32[64,128]{1,0:T(8,128)S(1)}, u32[]{:S(2)}, u32[]{:S(2)}) collective-permute-start(f32[64,128]{1,0:T(8,128)S(1)} %bitcast_multiply_fusion), channel_id=1, source_target_pairs={{0,4},{4,0},{8,12},{12,8},{16,20},{20,16},{24,28},{28,24},{1,5},{5... | collective-permute-start | bytes 98312 | tf_op jit(solution)/shard_map/ppermute | solution.py:18
  54.4 1.6 %collective-permute-done.5 = f32[64,128]{1,0:T(8,128)S(1)} collective-permute-done((f32[64,128]{1,0:T(8,128)S(1)}, f32[64,128]{1,0:T(8,128)S(1)}, u32[]{:S(2)}, u32[]{:S(2)}) %collective-permute-start.5) | collective-permute-done | bytes 32800 | tf_op jit(solution)/shard_map/ppermute | solution.py:18
  57.0 5.8 %cholesky.31 = f32[64,64]{1,0:T(8,128)S(1)} custom-call(f32[64,64]{1,0:T(8,128)S(1)} %fusion.57), custom_call_target="Cholesky" | custom-call | tf_op jit(solution)/shard_map/jit(cholesky)/cholesky | solution.py:39
  62.9 0.6 compare_reduce_fusion.1
  63.6 0.7 fusion.50
  64.2 4.9 %custom-call.20 = f32[1,64,64]{1,2,0:T(8,128)S(1)} custom-call(f32[1,64,64]{2,1,0:T(8,128)S(1)} %fusion.50), custom_call_target="InvertDiagBlocksLowerTriangular" | custom-call | tf_op jit(solution)/shard_map/jit(_cho_solve)/triangular_solve | solution.py:40
  70.2 0.4 fusion.13
  71.3 0.4 fusion.15
  73.2 1.1 gather_fusion.5
  74.4 0.5 collective-permute-start.4
  75.8 1.7 %gather_fusion.3 = f32[384,384]{1,0:T(8,128)S(1)} fusion(f32[384,384]{1,0:T(8,128)S(1)} %maximum_maximum_fusion, s32[1024]{0:T(1024)S(1)} %pad_clamp_fusion.2), kind=kCustom, calls=%fused_computation.5 | custom fusion | bytes 1181184 | tf_op jit(solution)/shard_map/jit(_take)/gather | solution.py:166
  77.9 1.9 %gather_fusion.4 = f32[384,384]{1,0:T(8,128)S(1)} fusion(f32[384,384]{0,1:T(8,128)S(1)} %broadcast_select_fusion, s32[1024]{0:T(1024)S(1)} %pad_clamp_fusion.2), kind=kCustom, calls=%fused_computation.6 | custom fusion | bytes 1181184 | tf_op jit(solution)/shard_map/jit(_take)/gather | solution.py:166
  80.2 0.5 collective-permute-start.2
  80.9 0.5 collective-permute-done.1
  82.1 11.7 %cholesky.65 = f32[128,128]{1,0:T(8,128)S(1)} custom-call(f32[128,128]{1,0:T(8,128)S(1)} %fusion.24), custom_call_target="Cholesky" | custom-call | tf_op jit(solution)/shard_map/jit(cholesky)/cholesky | solution.py:39
  93.8 0.6 compare_reduce_fusion
  94.5 0.7 fusion.17
  95.1 9.8 %custom-call.21 = f32[1,128,128]{1,2,0:T(8,128)S(1)} custom-call(f32[1,128,128]{2,1,0:T(8,128)S(1)} %fusion.17), custom_call_target="InvertDiagBlocksLowerTriangular" | custom-call | tf_op jit(solution)/shard_map/jit(_cho_solve)/triangular_solve | solution.py:40
  106.4 0.6 slice-done
  106.9 0.8 fusion.9
  110.7 0.7 gather_fusion.7
  111.6 0.7 copy.48
  112.5 1.1 fusion.2
  113.5 0.7 maximum_select_fusion
  (129 shorter events, 12.9 us)
Async XLA Ops:
  0.6 3.1 %copy-start = (f32[1,1,256,256]{3,2,1,0:T(8,128)S(1)}, f32[1,1,256,256]{3,2,1,0:T(8,128)}, u32[]{:S(2)}) copy-start(f32[1,1,256,256]{3,2,1,0:T(8,128)} %param.8) | copy-start | bytes 786436
  1.1 0.7 copy-start.1
  6.0 3.1 %copy-start.5 = (f32[1,1,64,256]{3,2,1,0:T(8,128)S(1)}, f32[1,1,64,256]{3,2,1,0:T(8,128)}, u32[]{:S(2)}) copy-start(f32[1,1,64,256]{3,2,1,0:T(8,128)} %param.9) | copy-start | bytes 196612
  6.1 50.1 %collective-permute-start = (f32[256,256]{1,0:T(8,128)S(1)}, f32[256,256]{1,0:T(8,128)S(1)}, u32[]{:S(2)}, u32[]{:S(2)}) collective-permute-start(f32[256,256]{1,0:T(8,128)S(1)} %select_bitcast_fusion.1), channel_id=1, source_target_pairs={{0,4},{4,0},{8,12},{12,8},{16,20},{20,16},{24,28},{28,24},{1,5},{5... | collective-permute-start | bytes 786440 | tf_op jit(solution)/shard_map/ppermute | solution.py:18
  10.0 0.8 copy-start.3
  10.1 46.0 %collective-permute-start.3 = (f32[64,256]{1,0:T(8,128)S(1)}, f32[64,256]{1,0:T(8,128)S(1)}, u32[]{:S(2)}, u32[]{:S(2)}) collective-permute-start(f32[64,256]{1,0:T(8,128)S(1)} %select_bitcast_fusion.4), channel_id=1, source_target_pairs={{0,4},{4,0},{8,12},{12,8},{16,20},{20,16},{24,28},{28,24},{1,5},{5... | collective-permute-start | bytes 196616 | tf_op jit(solution)/shard_map/ppermute | solution.py:18
  51.8 4.2 %collective-permute-start.5 = (f32[64,128]{1,0:T(8,128)S(1)}, f32[64,128]{1,0:T(8,128)S(1)}, u32[]{:S(2)}, u32[]{:S(2)}) collective-permute-start(f32[64,128]{1,0:T(8,128)S(1)} %bitcast_multiply_fusion), channel_id=1, source_target_pairs={{0,4},{4,0},{8,12},{12,8},{16,20},{20,16},{24,28},{28,24},{1,5},{5... | collective-permute-start | bytes 98312 | tf_op jit(solution)/shard_map/ppermute | solution.py:18
  56.0 52.8 %collective-permute-start.6 = (f32[64,256]{1,0:T(8,128)S(1)}, f32[64,256]{1,0:T(8,128)S(1)}, u32[]{:S(2)}, u32[]{:S(2)}) collective-permute-start(f32[64,256]{1,0:T(8,128)S(1)} %pad_maximum_fusion.1), channel_id=1, source_target_pairs={{0,1},{1,0},{2,3},{3,2},{4,5},{5,4},{6,7},{7,6},{8,9},{9,8},{10,11... | collective-permute-start | bytes 196616 | tf_op jit(solution)/shard_map/ppermute | solution.py:18
  74.4 6.3 %copy-start.2 = (f32[64,384]{1,0:T(8,128)}, f32[64,384]{1,0:T(8,128)S(1)}, u32[]{:S(2)}) copy-start(f32[64,384]{1,0:T(8,128)S(1)} %select_bitcast_fusion.3) | copy-start | bytes 294916
  74.4 6.3 %collective-permute-start.4 = (f32[64,128]{1,0:T(8,128)S(1)}, f32[64,128]{1,0:T(8,128)S(1)}, u32[]{:S(2)}, u32[]{:S(2)}) collective-permute-start(f32[64,128]{1,0:T(8,128)S(1)} %slice.152), channel_id=1, source_target_pairs={{0,1},{1,0},{2,3},{3,2},{4,5},{5,4},{6,7},{7,6},{8,9},{9,8},{10,11... | collective-permute-start | bytes 98312 | tf_op jit(solution)/shard_map/ppermute | solution.py:18
  80.1 1.3 %collective-permute-start.1 = (f32[128,128]{1,0:T(8,128)S(1)}, f32[128,128]{1,0:T(8,128)S(1)}, u32[]{:S(2)}, u32[]{:S(2)}) collective-permute-start(f32[128,128]{1,0:T(8,128)S(1)} %slice.145), channel_id=1, source_target_pairs={{0,1},{1,0},{2,3},{3,2},{4,5},{5,4},{6,7},{7,6},{8,9},{9,8},{10,11... | collective-permute-start | bytes 196616 | tf_op jit(solution)/shard_map/ppermute | solution.py:18
  80.2 27.8 %collective-permute-start.2 = (f32[256,128]{1,0:T(8,128)S(1)}, f32[256,128]{1,0:T(8,128)S(1)}, u32[]{:S(2)}, u32[]{:S(2)}) collective-permute-start(f32[256,128]{1,0:T(8,128)S(1)} %slice.144), channel_id=1, source_target_pairs={{0,1},{1,0},{2,3},{3,2},{4,5},{5,4},{6,7},{7,6},{8,9},{9,8},{10,11... | collective-permute-start | bytes 393224 | tf_op jit(solution)/shard_map/ppermute | solution.py:18
  106.1 0.8 slice-start
  111.6 0.9 copy-start.4
  111.6 0.9 copy-start.6
